TPU v7x, 32 devices: a whole 2x2x4 slice. The times are simulated.
32 devices in a mesh: query: 8 (over z, y), item: 4 (over x, core).
Axes of the slice: x: 2, y: 2, z: 4, core: 2. Of those that a mesh axis runs over, the one named last changes fastest.
Arguments:
- query_emb: bfloat16 [2048, 256], P(('query', 'item')), may hold values from -400 to 400
- targets: int32 [2048], P('query'), may hold values from 0 to 8191, as said below
- eligible_tiles: int32 [32, 32], P('query', 'item'), may hold values from 0 to 1, as said below
- item_feats: bfloat16 [4, 2048, 512], P('item', 'query'), may hold values from -6 to 6
- w_first: bfloat16 [512, 1024], replicated, may hold values from -0.25 to 0.25
- w_second: bfloat16 [1024, 256], replicated, may hold values from -0.1875 to 0.1875
Outputs:
- loss: float32 [2048], P(('query', 'item'))
- query_grad: float32 [2048, 256], P(('query', 'item'))
- w_first_grad: float32 [512, 1024], replicated
- w_second_grad: float32 [1024, 256], replicated
Inputs may be any that keep to these rules, and one draw needn't show every extreme that they name: `eligible_tiles`: every row has at least one 1. The block targets[q] // 256 is marked 1 in row q // 64 of eligible_tiles.
All inputs are finite; a program needn't handle non-finite values.
Results may differ from a plain program's by a relative error of at most 0.007.
Values may be sent and summed in bfloat16 or wider, within the bound.
A program may use at most 64 MiB of HBM per device.

v0:
```python
import math
import jax
import jax.numpy as jnp
from jax import lax
from jax.sharding import PartitionSpec as P


def passed_along(x, axis, by):
    count = lax.axis_size(axis)
    return lax.ppermute(x, axis, [(i, (i + by) % count) for i in range(count)])


def expand_blocks(block_flags, per_block):
    widened = jnp.broadcast_to((block_flags > 0)[..., None], block_flags.shape + (per_block,))
    return widened.reshape(block_flags.shape[:-1] + (block_flags.shape[-1] * per_block,))


def tile_scores(queries, item_tile):
    return 0.25 * jnp.einsum("qe,ie->qi", queries, item_tile, preferred_element_type=jnp.float32)


def on_device(query_emb, targets, eligible_tiles, item_feats, w_first, w_second):
    q_rows = query_emb.shape[0]
    item_count = lax.axis_size("item")
    query_count = lax.axis_size("query")
    item_pos = lax.axis_index("item")
    tokens = item_feats.reshape(item_feats.shape[1], item_feats.shape[2])
    block_rows = tokens.shape[0]
    pre_act = jnp.dot(tokens, w_first, preferred_element_type=jnp.float32)
    hidden = jax.nn.silu(pre_act).astype(jnp.bfloat16)
    own_emb = jnp.dot(hidden, w_second, preferred_element_type=jnp.float32).astype(jnp.bfloat16)
    item_tile = lax.all_gather(own_emb, "query", axis=0, tiled=True)
    tile_rows = item_tile.shape[0]
    emb_width = item_tile.shape[1]
    columns = jnp.arange(tile_rows, dtype=jnp.int32)
    first_item = item_pos * tile_rows
    start_cache = jnp.zeros((1, 1, 1), jnp.bfloat16)

    def forward_step(step_idx, carried):
        visitor, run_max, run_sum, positive, seen = carried
        anchor = (item_pos - step_idx) % item_count
        live_cols = expand_blocks(
            lax.dynamic_index_in_dim(eligible_tiles, anchor, 0, keepdims=False), block_rows
        )[None, :]
        wanted = lax.dynamic_slice_in_dim(targets, anchor * q_rows, q_rows, 0) - first_item
        queries = visitor.astype(jnp.bfloat16)
        scores = tile_scores(queries, item_tile)
        masked = jnp.where(live_cols, scores, -1e30)
        new_max = jnp.maximum(run_max, jnp.max(masked, axis=1))
        added = jnp.sum(jnp.where(live_cols, jnp.exp(masked - new_max[:, None]), 0.0), axis=1)
        run_sum = run_sum * jnp.exp(run_max - new_max) + added
        positive = positive + jnp.sum(
            jnp.where(columns[None, :] == wanted[:, None], scores, 0.0), axis=1
        )
        moved = passed_along((visitor, new_max, run_sum, positive), "item", 1)
        return (moved[0], moved[1], moved[2], moved[3], seen)

    start_state = (
        query_emb.astype(jnp.float32),
        jnp.full((q_rows,), -1e30, jnp.float32),
        jnp.zeros((q_rows,), jnp.float32),
        jnp.zeros((q_rows,), jnp.float32),
        start_cache,
    )
    visitor, run_max, run_sum, positive, seen = lax.fori_loop(
        0, item_count, forward_step, start_state
    )
    log_norm = run_max + jnp.log(run_sum)
    loss = log_norm - positive

    def tile_grads(queries, norm_here, step_idx):
        anchor = (item_pos - step_idx) % item_count
        live_cols = expand_blocks(
            lax.dynamic_index_in_dim(eligible_tiles, anchor, 0, keepdims=False), block_rows
        )[None, :]
        wanted = lax.dynamic_slice_in_dim(targets, anchor * q_rows, q_rows, 0) - first_item
        masked = jnp.where(live_cols, tile_scores(queries, item_tile), -1e30)
        softmax_w = jnp.where(live_cols, jnp.exp(masked - norm_here[:, None]), 0.0)
        coeffs = (softmax_w - (columns[None, :] == wanted[:, None]).astype(jnp.float32)).astype(
            jnp.bfloat16
        )
        q_part = 0.25 * jnp.dot(coeffs, item_tile, preferred_element_type=jnp.float32)
        e_part = 0.25 * jnp.einsum("qi,qe->ie", coeffs, queries, preferred_element_type=jnp.float32)
        return (q_part, e_part)

    zero_q = jnp.zeros((q_rows, emb_width), jnp.float32)
    zero_e = jnp.zeros(item_tile.shape, jnp.float32)

    def backward_step(step_idx, carried):
        travel, emb_grad = carried
        visitor, norm_here, q_grads = travel
        q_part, e_part = tile_grads(visitor.astype(jnp.bfloat16), norm_here, step_idx)
        travel = passed_along((visitor, norm_here, q_grads + q_part), "item", 1)
        return (travel, emb_grad + e_part)

    start_back = ((query_emb.astype(jnp.float32), log_norm, zero_q), zero_e)
    travel, emb_grad = lax.fori_loop(0, item_count, backward_step, start_back)
    query_grad = travel[2]
    own_grad = lax.psum_scatter(emb_grad, "query", scatter_dimension=0, tiled=True).astype(
        jnp.bfloat16
    )
    second_term = jnp.einsum("ih,ie->he", hidden, own_grad, preferred_element_type=jnp.float32)
    hid_grad = jnp.einsum("ie,he->ih", own_grad, w_second, preferred_element_type=jnp.float32)
    gate_sig = jax.nn.sigmoid(pre_act)
    pre_grad = (hid_grad * gate_sig * (1.0 + pre_act * (1.0 - gate_sig))).astype(jnp.bfloat16)
    first_term = jnp.einsum("id,ih->dh", tokens, pre_grad, preferred_element_type=jnp.float32)
    tower_sums = lax.psum((first_term, second_term), ("query", "item"))
    grad_scale = 1.0 / math.sqrt(block_rows * query_count * item_count)
    return (loss, query_grad, tower_sums[0] * grad_scale, tower_sums[1] * grad_scale)


def solution(mesh):
    return jax.shard_map(
        on_device,
        mesh=mesh,
        in_specs=(
            P(("query", "item"), None),
            P("query"),
            P("query", "item"),
            P("item", "query", None),
            P(),
            P(),
        ),
        out_specs=(P(("query", "item")), P(("query", "item"), None), P(), P()),
        check_vma=False,
    )
```

profile of v0, /device:TPU:0, one launch (start us, length us, event | category | flops | bytes accessed | tf_op | source)
XLA Modules:
  0.0 334.7 jit_solution(5722697712973858926)
XLA Ops:
  7.2 0.9 copy.45
  8.4 1.4 fusion.22
  9.8 1.0 copy-done.2
  10.8 1.1 convolution_convert_fusion
  12.0 42.9 %all-gather.2.cloned.1.call-done = bf16[2048,256]{1,0:T(8,128)(2,1)} async-done(((bf16[256,256]{1,0:T(8,128)(2,1)}), bf16[2048,256]{1,0:T(8,128)(2,1)}) %all-gather.2.cloned.1.call-update) | async-done | bytes 1048592 | tf_op jit(solution)/shard_map/all_gather | solution.py:32
  54.9 26.8 %while.44 = (s32[]{:T(128)}, bf16[64,256]{1,0:T(8,128)(2,1)S(1)}, f32[64]{0:T(128)S(1)}, f32[64]{0:T(128)S(1)}, f32[64]{0:T(128)S(1)}, /*index=5*/s32[]{:T(128)}...) while((s32[]{:T(128)}, bf16[64,256]{1,0:T(8,128)(2,1)S(1)}, ...), condition=%wide.region_4.5_spmd.clone, body=%wide.region_0.4_spmd.clone.sunk | while | flops 68419800 | bytes 2345530 | solution.py:65
  55.1 1.8 select_reduce_fusion.5
  56.9 1.6 collective-permute-start.1
  59.0 0.6 collective-permute-start.3
  59.9 2.0 collective-permute-done.2
  62.3 1.8 select_reduce_fusion.5
  64.1 0.7 collective-permute-start.1
  65.3 1.5 collective-permute-start.3
  67.1 1.1 collective-permute-done.2
  68.5 1.8 select_reduce_fusion.5
  70.3 1.6 collective-permute-start.1
  72.0 0.3 select_reduce_fusion.6
  72.4 0.6 collective-permute-start.3
  73.3 2.0 collective-permute-done.2
  75.7 1.8 select_reduce_fusion.5
  77.4 0.7 collective-permute-start.1
  78.2 0.3 select_reduce_fusion.6
  78.6 1.5 collective-permute-start.3
  80.5 1.1 collective-permute-done.2
  81.7 0.5 fusion.29
  82.3 29.5 %while.45 = (s32[]{:T(128)}, bf16[64,256]{1,0:T(8,128)(2,1)S(1)}, f32[64]{0:T(128)S(1)}, f32[64,256]{1,0:T(8,128)S(1)}, f32[2048,256]{1,0:T(8,128)}, /*index=5*/...) while((s32[]{:T(128)}, bf16[64,256]{1,0:T(8,128)(2,1)S(1)}, ...), condition=%wide.region_6.7_spmd.clone, body=%wide.region_5.6_spmd.clone.sunk | while | flops 203980896 | bytes 11938872 | solution.py:97
  82.4 1.6 collective-permute-start.5
  84.1 1.7 fusion.60
  86.2 1.8 fusion.62
  88.0 1.8 collective-permute-done.6
  89.9 0.7 collective-permute-start.5
  90.7 1.7 fusion.60
  92.9 3.4 %fusion.62 = f32[2048,256]{1,0:T(8,128)} fusion(bf16[64,2048]{1,0:T(8,128)(2,1)S(1)} %fusion.60, f32[2048,256]{1,0:T(8,128)} %get-tuple-element.849, pred[]{:T(512)S(6)} %compare.5, bf16[64,256]{1,0:T(8,128)(2,1)S(1)} %copy.32), kind=kOutput, calls=%fused_computation.12.clone.1 | convolution fusion | flops 68681728 | bytes 4489217 | tf_op jit(solution)/shard_map/while/body/eval_jaxpr/qi,qe->ie/dot_general | solution.py:83
  96.5 1.4 collective-permute-start.4
  98.3 1.7 fusion.60
  100.3 0.5 collective-permute-start.6
  100.8 3.4 %fusion.62 = f32[2048,256]{1,0:T(8,128)} fusion(bf16[64,2048]{1,0:T(8,128)(2,1)S(1)} %fusion.60, f32[2048,256]{1,0:T(8,128)} %get-tuple-element.849, pred[]{:T(512)S(6)} %compare.5, bf16[64,256]{1,0:T(8,128)(2,1)S(1)} %copy.32), kind=kOutput, calls=%fused_computation.12.clone.1 | convolution fusion | flops 68681728 | bytes 4489217 | tf_op jit(solution)/shard_map/while/body/eval_jaxpr/qi,qe->ie/dot_general | solution.py:83
  104.5 1.4 collective-permute-start.5
  106.0 1.7 fusion.60
  108.3 3.4 %fusion.62 = f32[2048,256]{1,0:T(8,128)} fusion(bf16[64,2048]{1,0:T(8,128)(2,1)S(1)} %fusion.60, f32[2048,256]{1,0:T(8,128)} %get-tuple-element.849, pred[]{:T(512)S(6)} %compare.5, bf16[64,256]{1,0:T(8,128)(2,1)S(1)} %copy.32), kind=kOutput, calls=%fused_computation.12.clone.1 | convolution fusion | flops 68681728 | bytes 4489217 | tf_op jit(solution)/shard_map/while/body/eval_jaxpr/qi,qe->ie/dot_general | solution.py:83
  111.8 66.9 %reduce-scatter.2.cloned.1.call-done = f32[256,256]{1,0:T(8,128)} async-done(((f32[2048,256]{1,0:T(8,128)}), f32[256,256]{1,0:T(8,128)}) %reduce-scatter.2.cloned.1.call-update) | async-done | bytes 262160 | tf_op jit(solution)/shard_map/reduce_scatter | solution.py:99
  178.7 3.2 convolution_bitcast_fusion
  181.9 1.5 fusion.24
  183.4 138.1 %all-reduce.3.cloned.1.call-done = (f32[512,1024]{0,1:T(8,128)}, f32[1024,256]{1,0:T(8,128)}) async-done(((f32[512,1024]{0,1:T(8,128)}, f32[1024,256]{1,0:T(8,128)}), (f32[512,1024]{0,1:T(8,128)}, f32[1024,256]{1,0:T(8,128)})) %all-reduce.3.cloned.1.call-update) | async-done | bytes 3145744 | tf_op jit(solution)/shard_map/psum | solution.py:107
  321.6 1.8 broadcast_multiply_fusion
  323.4 1.8 copy.10
  325.2 2.3 broadcast_multiply_fusion.1
  327.5 0.6 copy.46
  (139 shorter events, 7.5 us)
Async XLA Ops:
  7.2 1.2 copy-start
  7.2 3.6 %copy-start.6 = (bf16[1024,256]{1,0:T(8,128)(2,1)S(1)}, bf16[1024,256]{1,0:T(8,128)(2,1)}, u32[]{:S(2)}) copy-start(bf16[1024,256]{1,0:T(8,128)(2,1)} %param.15) | copy-start | bytes 1572868
  7.2 47.7 %all-gather.2.cloned.1.call-start = ((), (), s32[]{:S(2)}) async-start(), calls=%async_computation.1 | async-start | bytes 1179648 | tf_op jit(solution)/shard_map/all_gather | solution.py:32
  9.8 1.0 copy-start.2
  10.8 44.1 %copy-start.5 = (s32[256]{0:T(256)S(1)}, s32[256]{0:T(256)}, u32[]{:S(2)}) copy-start(s32[256]{0:T(256)} %param.11) | copy-start | bytes 3076
  10.8 44.1 %copy-start.8 = (s32[4,8]{1,0:T(4,128)S(1)}, s32[4,8]{1,0:T(4,128)}, u32[]{:S(2)}) copy-start(s32[4,8]{1,0:T(4,128)} %param.12) | copy-start | bytes 388
  11.9 166.8 %reduce-scatter.2.cloned.1.call-start = ((), (), s32[]{:S(2)}) async-start(), calls=%async_computation.2 | async-start | bytes 2359296 | tf_op jit(solution)/shard_map/reduce_scatter | solution.py:99
  54.9 7.2 %collective-permute-start = (bf16[64,256]{1,0:T(8,128)(2,1)S(1)}, bf16[64,256]{1,0:T(8,128)(2,1)S(1)}, u32[]{:S(2)}, u32[]{:S(2)}) collective-permute-start(bf16[64,256]{1,0:T(8,128)(2,1)S(1)} %copy.17), channel_id=1, source_target_pairs={{0,1},{1,2},{2,3},{3,0},{4,5},{5,6},{6,7},{7,4},{8,9},{9,10},{10,1... | collective-permute-start | bytes 98312 | tf_op jit(solution)/shard_map/while/body/eval_jaxpr/ppermute | solution.py:10
  56.9 3.0 collective-permute-start.1
  58.9 3.0 collective-permute-start.2
  59.0 3.1 collective-permute-start.3
  62.1 6.2 %collective-permute-start = (bf16[64,256]{1,0:T(8,128)(2,1)S(1)}, bf16[64,256]{1,0:T(8,128)(2,1)S(1)}, u32[]{:S(2)}, u32[]{:S(2)}) collective-permute-start(bf16[64,256]{1,0:T(8,128)(2,1)S(1)} %copy.17), channel_id=1, source_target_pairs={{0,1},{1,2},{2,3},{3,0},{4,5},{5,6},{6,7},{7,4},{8,9},{9,10},{10,1... | collective-permute-start | bytes 98312 | tf_op jit(solution)/shard_map/while/body/eval_jaxpr/ppermute | solution.py:10
  64.1 3.0 collective-permute-start.1
  65.2 3.0 collective-permute-start.2
  65.3 3.1 collective-permute-start.3
  68.4 7.1 %collective-permute-start = (bf16[64,256]{1,0:T(8,128)(2,1)S(1)}, bf16[64,256]{1,0:T(8,128)(2,1)S(1)}, u32[]{:S(2)}, u32[]{:S(2)}) collective-permute-start(bf16[64,256]{1,0:T(8,128)(2,1)S(1)} %copy.17), channel_id=1, source_target_pairs={{0,1},{1,2},{2,3},{3,0},{4,5},{5,6},{6,7},{7,4},{8,9},{9,10},{10,1... | collective-permute-start | bytes 98312 | tf_op jit(solution)/shard_map/while/body/eval_jaxpr/ppermute | solution.py:10
  70.3 3.0 collective-permute-start.1
  72.3 3.0 collective-permute-start.2
  72.4 3.1 collective-permute-start.3
  75.5 6.2 %collective-permute-start = (bf16[64,256]{1,0:T(8,128)(2,1)S(1)}, bf16[64,256]{1,0:T(8,128)(2,1)S(1)}, u32[]{:S(2)}, u32[]{:S(2)}) collective-permute-start(bf16[64,256]{1,0:T(8,128)(2,1)S(1)} %copy.17), channel_id=1, source_target_pairs={{0,1},{1,2},{2,3},{3,0},{4,5},{5,6},{6,7},{7,4},{8,9},{9,10},{10,1... | collective-permute-start | bytes 98312 | tf_op jit(solution)/shard_map/while/body/eval_jaxpr/ppermute | solution.py:10
  77.4 3.0 collective-permute-start.1
  78.6 3.0 collective-permute-start.2
  78.6 3.1 collective-permute-start.3
  82.3 3.5 %copy-start.1 = (bf16[2048,256]{1,0:T(8,128)(2,1)S(1)}, bf16[2048,256]{1,0:T(8,128)(2,1)}, u32[]{:S(2)}) copy-start(bf16[2048,256]{1,0:T(8,128)(2,1)} %get-tuple-element.868) | copy-start | bytes 3145732 | tf_op jit(solution)/shard_map/while
  82.3 5.8 %collective-permute-start.4 = (bf16[64,256]{1,0:T(8,128)(2,1)S(1)}, bf16[64,256]{1,0:T(8,128)(2,1)S(1)}, u32[]{:S(2)}, u32[]{:S(2)}) collective-permute-start(bf16[64,256]{1,0:T(8,128)(2,1)S(1)} %copy.32), channel_id=1, source_target_pairs={{0,1},{1,2},{2,3},{3,0},{4,5},{5,6},{6,7},{7,4},{8,9},{9,10},{10,1... | collective-permute-start | bytes 98312 | tf_op jit(solution)/shard_map/while/body/eval_jaxpr/ppermute | solution.py:10
  82.4 5.7 %collective-permute-start.5 = (f32[64]{0:T(128)S(1)}, f32[64]{0:T(128)S(1)}, u32[]{:S(2)}, u32[]{:S(2)}) collective-permute-start(f32[64]{0:T(128)S(1)} %copy.33), channel_id=1, source_target_pairs={{0,1},{1,2},{2,3},{3,0},{4,5},{5,6},{6,7},{7,4},{8,9},{9,10},{10,1... | collective-permute-start | bytes 776 | tf_op jit(solution)/shard_map/while/body/eval_jaxpr/ppermute | solution.py:10
  86.1 3.7 %collective-permute-start.6 = (f32[64,256]{1,0:T(8,128)S(1)}, f32[64,256]{1,0:T(8,128)S(1)}, u32[]{:S(2)}, u32[]{:S(2)}) collective-permute-start(f32[64,256]{1,0:T(8,128)S(1)} %fusion.61), channel_id=1, source_target_pairs={{0,1},{1,2},{2,3},{3,0},{4,5},{5,6},{6,7},{7,4},{8,9},{9,10},{10,1... | collective-permute-start | bytes 196616 | tf_op jit(solution)/shard_map/while/body/eval_jaxpr/ppermute | solution.py:10
  89.9 2.6 copy-start.1
  89.9 6.4 %collective-permute-start.4 = (bf16[64,256]{1,0:T(8,128)(2,1)S(1)}, bf16[64,256]{1,0:T(8,128)(2,1)S(1)}, u32[]{:S(2)}, u32[]{:S(2)}) collective-permute-start(bf16[64,256]{1,0:T(8,128)(2,1)S(1)} %copy.32), channel_id=1, source_target_pairs={{0,1},{1,2},{2,3},{3,0},{4,5},{5,6},{6,7},{7,4},{8,9},{9,10},{10,1... | collective-permute-start | bytes 98312 | tf_op jit(solution)/shard_map/while/body/eval_jaxpr/ppermute | solution.py:10
  89.9 6.4 %collective-permute-start.5 = (f32[64]{0:T(128)S(1)}, f32[64]{0:T(128)S(1)}, u32[]{:S(2)}, u32[]{:S(2)}) collective-permute-start(f32[64]{0:T(128)S(1)} %copy.33), channel_id=1, source_target_pairs={{0,1},{1,2},{2,3},{3,0},{4,5},{5,6},{6,7},{7,4},{8,9},{9,10},{10,1... | collective-permute-start | bytes 776 | tf_op jit(solution)/shard_map/while/body/eval_jaxpr/ppermute | solution.py:10
  92.7 3.7 %collective-permute-start.6 = (f32[64,256]{1,0:T(8,128)S(1)}, f32[64,256]{1,0:T(8,128)S(1)}, u32[]{:S(2)}, u32[]{:S(2)}) collective-permute-start(f32[64,256]{1,0:T(8,128)S(1)} %fusion.61), channel_id=1, source_target_pairs={{0,1},{1,2},{2,3},{3,0},{4,5},{5,6},{6,7},{7,4},{8,9},{9,10},{10,1... | collective-permute-start | bytes 196616 | tf_op jit(solution)/shard_map/while/body/eval_jaxpr/ppermute | solution.py:10
  96.5 3.5 %copy-start.1 = (bf16[2048,256]{1,0:T(8,128)(2,1)S(1)}, bf16[2048,256]{1,0:T(8,128)(2,1)}, u32[]{:S(2)}) copy-start(bf16[2048,256]{1,0:T(8,128)(2,1)} %get-tuple-element.868) | copy-start | bytes 3145732 | tf_op jit(solution)/shard_map/while
  96.5 7.7 %collective-permute-start.4 = (bf16[64,256]{1,0:T(8,128)(2,1)S(1)}, bf16[64,256]{1,0:T(8,128)(2,1)S(1)}, u32[]{:S(2)}, u32[]{:S(2)}) collective-permute-start(bf16[64,256]{1,0:T(8,128)(2,1)S(1)} %copy.32), channel_id=1, source_target_pairs={{0,1},{1,2},{2,3},{3,0},{4,5},{5,6},{6,7},{7,4},{8,9},{9,10},{10,1... | collective-permute-start | bytes 98312 | tf_op jit(solution)/shard_map/while/body/eval_jaxpr/ppermute | solution.py:10
  97.8 6.3 %collective-permute-start.5 = (f32[64]{0:T(128)S(1)}, f32[64]{0:T(128)S(1)}, u32[]{:S(2)}, u32[]{:S(2)}) collective-permute-start(f32[64]{0:T(128)S(1)} %copy.33), channel_id=1, source_target_pairs={{0,1},{1,2},{2,3},{3,0},{4,5},{5,6},{6,7},{7,4},{8,9},{9,10},{10,1... | collective-permute-start | bytes 776 | tf_op jit(solution)/shard_map/while/body/eval_jaxpr/ppermute | solution.py:10
  100.3 3.9 %collective-permute-start.6 = (f32[64,256]{1,0:T(8,128)S(1)}, f32[64,256]{1,0:T(8,128)S(1)}, u32[]{:S(2)}, u32[]{:S(2)}) collective-permute-start(f32[64,256]{1,0:T(8,128)S(1)} %fusion.61), channel_id=1, source_target_pairs={{0,1},{1,2},{2,3},{3,0},{4,5},{5,6},{6,7},{7,4},{8,9},{9,10},{10,1... | collective-permute-start | bytes 196616 | tf_op jit(solution)/shard_map/while/body/eval_jaxpr/ppermute | solution.py:10
  104.2 3.5 %copy-start.1 = (bf16[2048,256]{1,0:T(8,128)(2,1)S(1)}, bf16[2048,256]{1,0:T(8,128)(2,1)}, u32[]{:S(2)}) copy-start(bf16[2048,256]{1,0:T(8,128)(2,1)} %get-tuple-element.868) | copy-start | bytes 3145732 | tf_op jit(solution)/shard_map/while
  104.2 7.5 %collective-permute-start.4 = (bf16[64,256]{1,0:T(8,128)(2,1)S(1)}, bf16[64,256]{1,0:T(8,128)(2,1)S(1)}, u32[]{:S(2)}, u32[]{:S(2)}) collective-permute-start(bf16[64,256]{1,0:T(8,128)(2,1)S(1)} %copy.32), channel_id=1, source_target_pairs={{0,1},{1,2},{2,3},{3,0},{4,5},{5,6},{6,7},{7,4},{8,9},{9,10},{10,1... | collective-permute-start | bytes 98312 | tf_op jit(solution)/shard_map/while/body/eval_jaxpr/ppermute | solution.py:10
  104.5 7.2 %collective-permute-start.5 = (f32[64]{0:T(128)S(1)}, f32[64]{0:T(128)S(1)}, u32[]{:S(2)}, u32[]{:S(2)}) collective-permute-start(f32[64]{0:T(128)S(1)} %copy.33), channel_id=1, source_target_pairs={{0,1},{1,2},{2,3},{3,0},{4,5},{5,6},{6,7},{7,4},{8,9},{9,10},{10,1... | collective-permute-start | bytes 776 | tf_op jit(solution)/shard_map/while/body/eval_jaxpr/ppermute | solution.py:10
  108.0 3.7 %collective-permute-start.6 = (f32[64,256]{1,0:T(8,128)S(1)}, f32[64,256]{1,0:T(8,128)S(1)}, u32[]{:S(2)}, u32[]{:S(2)}) collective-permute-start(f32[64,256]{1,0:T(8,128)S(1)} %fusion.61), channel_id=1, source_target_pairs={{0,1},{1,2},{2,3},{3,0},{4,5},{5,6},{6,7},{7,4},{8,9},{9,10},{10,1... | collective-permute-start | bytes 196616 | tf_op jit(solution)/shard_map/while/body/eval_jaxpr/ppermute | solution.py:10
  111.8 66.9 %copy-start.3 = (f32[256,1024]{1,0:T(8,128)S(1)}, f32[256,1024]{1,0:T(8,128)}, u32[]{:S(2)}) copy-start(f32[256,1024]{1,0:T(8,128)} %copy-done.2) | copy-start | bytes 3145732
  111.8 66.9 %copy-start.4 = (bf16[1,256,512]{2,1,0:T(8,128)(2,1)S(1)}, bf16[1,256,512]{2,1,0:T(8,128)(2,1)}, u32[]{:S(2)}) copy-start(bf16[1,256,512]{2,1,0:T(8,128)(2,1)} %param.13) | copy-start | bytes 786436
  111.8 209.8 %all-reduce.3.cloned.1.call-start = ((), (), s32[]{:S(2)}) async-start(), calls=%async_computation.3 | async-start | bytes 6291456 | tf_op jit(solution)/shard_map/psum | solution.py:107
  178.7 3.2 copy-start.7
Sparse Core Ops, SparseCore 0:
  12.0 42.8 all-gather.1
  111.9 66.7 reduce-scatter.1
  184.8 136.6 all-reduce.2
where the time goes:
time: 335 us
  waiting for transfers between devices  258 us (77%)
  matrix products  34.1 us (10%)
  starting transfers between devices  16 us (5%)
  between operations  13.8 us (4%)
  other arithmetic  6.81 us (2%)
  local copies, waits for them, and re-layouts  5.39 us (2%)
    psum x1, waiting for transfers between devices, on_device(): tower_sums = lax.psum((first_term, second_term), ('query', 'item'))  138 us
    reduce_scatter x1, waiting for transfers between devices, on_device(): lax.psum_scatter(emb_grad, 'query', scatter_dimension=0, tiled=True)  66.9 us
    all_gather x1, waiting for transfers between devices, on_device(): item_tile = lax.all_gather(own_emb, 'query', axis=0, tiled=True)  42.9 us
    ppermute x28, starting transfers between devices, passed_along(): return lax.ppermute(x, axis, [(i, (i + by) % count) for i in range(count)])  15.9 us
    dot_general x8, matrix products, tile_scores(): jnp.einsum('qe,ie->qi', queries, item_tile, preferred_element_type=jnp.fl...  13.8 us
    dot_general x4, matrix products, tile_grads(): jnp.einsum('qi,qe->ie', coeffs, queries, preferred_element_type=jnp.float32)  11.9 us
    ppermute x28, waiting for transfers between devices, passed_along(): return lax.ppermute(x, axis, [(i, (i + by) % count) for i in range(count)])  10.1 us
  transfers between devices with their start and end apart: 31, of which 18 were waited for; matrix products, arithmetic and copies ran while one was open for 9% of the time, Pallas kernels for 0%

commit v1 on v0

--- a/solution.py
+++ b/solution.py
@@ -29,7 +29,14 @@
     pre_act = jnp.dot(tokens, w_first, preferred_element_type=jnp.float32)
     hidden = jax.nn.silu(pre_act).astype(jnp.bfloat16)
     own_emb = jnp.dot(hidden, w_second, preferred_element_type=jnp.float32).astype(jnp.bfloat16)
-    item_tile = lax.all_gather(own_emb, "query", axis=0, tiled=True)
+    size = lax.axis_size("query")
+    right = [(i_2, (i_2 + 1) % size) for i_2 in range(size)]
+    parts = [own_emb]
+    for far in range(1, size):
+        parts = [lax.ppermute(parts[0], "query", right), *parts]
+    whole = jnp.concatenate(parts, axis=0)
+    places = (lax.axis_index("query") + 1) * parts[-1].shape[0]
+    item_tile = jnp.roll(whole, places, axis=0)
     tile_rows = item_tile.shape[0]
     emb_width = item_tile.shape[1]
     columns = jnp.arange(tile_rows, dtype=jnp.int32)

time: 335 us -> 339 us (1.012)
  matrix products: 34.1 us -> 23.6 us
  waiting for transfers between devices: 258 us -> 267 us
    ppermute x0 -> x7, waiting for transfers between devices: none -> 53.6 us  [on_device(): parts = [lax.ppermute(parts[0], 'query', right), *parts]]
    all_gather x1 -> x0, waiting for transfers between devices: 42.9 us -> none  [on_device(): item_tile = lax.all_gather(own_emb, 'query', axis=0, tiled=True)]
    dot_general x8, matrix products: 13.8 us -> 4.01 us  [tile_scores(): jnp.einsum('qe,ie->qi', queries, item_tile, preferred_element_type=jnp.fl...]
  transfers between devices with their start and end apart: 31 -> 37, of which waited for: 18 -> 25; matrix products, arithmetic and copies ran while one was open for 9% -> 6% of each run, Pallas kernels for 0% -> 0%
where the time goes in v1:
time: 339 us
  waiting for transfers between devices  267 us (79%)
  matrix products  23.6 us (7%)
  starting transfers between devices  19.2 us (6%)
  between operations  14.3 us (4%)
  other arithmetic  6.91 us (2%)
  local copies, waits for them, and re-layouts  6.82 us (2%)
    psum x1, waiting for transfers between devices, on_device(): tower_sums = lax.psum((first_term, second_term), ('query', 'item'))  138 us
    reduce_scatter x1, waiting for transfers between devices, on_device(): lax.psum_scatter(emb_grad, 'query', scatter_dimension=0, tiled=True)  65.3 us
    ppermute x7, waiting for transfers between devices, on_device(): parts = [lax.ppermute(parts[0], 'query', right), *parts]  53.6 us
    ppermute x28, starting transfers between devices, passed_along(): return lax.ppermute(x, axis, [(i, (i + by) % count) for i in range(count)])  16.1 us
    dot_general x4, matrix products, tile_grads(): jnp.einsum('qi,qe->ie', coeffs, queries, preferred_element_type=jnp.float32)  11.9 us
    ppermute x28, waiting for transfers between devices, passed_along(): return lax.ppermute(x, axis, [(i, (i + by) % count) for i in range(count)])  10.3 us
  transfers between devices with their start and end apart: 37, of which 25 were waited for; matrix products, arithmetic and copies ran while one was open for 6% of the time, Pallas kernels for 0%

profile of v1, /device:TPU:0, one launch (start us, length us, event | category | flops | bytes accessed | tf_op | source)
XLA Modules:
  0.0 338.6 jit_solution(9566673776664694384)
XLA Ops:
  7.2 0.9 copy.60
  8.4 1.4 fusion.22
  9.8 0.4 convolution_convert_fusion
  10.3 0.5 copy-done.4
  10.8 3.0 collective-permute-start.7
  13.8 6.5 %collective-permute-done.7 = bf16[256,256]{1,0:T(8,128)(2,1)S(1)} collective-permute-done((bf16[256,256]{1,0:T(8,128)(2,1)S(1)}, bf16[256,256]{1,0:T(8,128)(2,1)S(1)}, u32[]{:S(2)}, u32[]{:S(2)}) %collective-permute-start.7) | collective-permute-done | bytes 131104 | tf_op jit(solution)/shard_map/ppermute | solution.py:36
  20.3 7.7 %collective-permute-done.8 = bf16[256,256]{1,0:T(8,128)(2,1)S(1)} collective-permute-done((bf16[256,256]{1,0:T(8,128)(2,1)S(1)}, bf16[256,256]{1,0:T(8,128)(2,1)S(1)}, u32[]{:S(2)}, u32[]{:S(2)}) %collective-permute-start.8) | collective-permute-done | bytes 131104 | tf_op jit(solution)/shard_map/ppermute | solution.py:36
  28.0 7.7 %collective-permute-done.9 = bf16[256,256]{1,0:T(8,128)(2,1)S(1)} collective-permute-done((bf16[256,256]{1,0:T(8,128)(2,1)S(1)}, bf16[256,256]{1,0:T(8,128)(2,1)S(1)}, u32[]{:S(2)}, u32[]{:S(2)}) %collective-permute-start.9) | collective-permute-done | bytes 131104 | tf_op jit(solution)/shard_map/ppermute | solution.py:36
  35.6 7.7 %collective-permute-done.10 = bf16[256,256]{1,0:T(8,128)(2,1)S(1)} collective-permute-done((bf16[256,256]{1,0:T(8,128)(2,1)S(1)}, bf16[256,256]{1,0:T(8,128)(2,1)S(1)}, u32[]{:S(2)}, u32[]{:S(2)}) %collective-permute-start.10) | collective-permute-done | bytes 131104 | tf_op jit(solution)/shard_map/ppermute | solution.py:36
  43.3 7.7 %collective-permute-done.11 = bf16[256,256]{1,0:T(8,128)(2,1)S(1)} collective-permute-done((bf16[256,256]{1,0:T(8,128)(2,1)S(1)}, bf16[256,256]{1,0:T(8,128)(2,1)S(1)}, u32[]{:S(2)}, u32[]{:S(2)}) %collective-permute-start.11) | collective-permute-done | bytes 131104 | tf_op jit(solution)/shard_map/ppermute | solution.py:36
  51.0 8.8 %collective-permute-done.12 = bf16[256,256]{1,0:T(8,128)(2,1)S(1)} collective-permute-done((bf16[256,256]{1,0:T(8,128)(2,1)S(1)}, bf16[256,256]{1,0:T(8,128)(2,1)S(1)}, u32[]{:S(2)}, u32[]{:S(2)}) %collective-permute-start.12) | collective-permute-done | bytes 131104 | tf_op jit(solution)/shard_map/ppermute | solution.py:36
  59.8 7.7 %collective-permute-done.13 = bf16[256,256]{1,0:T(8,128)(2,1)S(1)} collective-permute-done((bf16[256,256]{1,0:T(8,128)(2,1)S(1)}, bf16[256,256]{1,0:T(8,128)(2,1)S(1)}, u32[]{:S(2)}, u32[]{:S(2)}) %collective-permute-start.13) | collective-permute-done | bytes 131104 | tf_op jit(solution)/shard_map/ppermute | solution.py:36
  67.9 0.5 copy-done.3
  68.4 21.9 %while.44 = (s32[]{:T(128)}, bf16[64,256]{1,0:T(8,128)(2,1)S(1)}, f32[64]{0:T(128)S(1)}, f32[64]{0:T(128)S(1)}, f32[64]{0:T(128)S(1)}, /*index=5*/s32[]{:T(128)}...) while((s32[]{:T(128)}, bf16[64,256]{1,0:T(8,128)(2,1)S(1)}, ...), condition=%wide.region_4.5_spmd.clone, body=%wide.region_0.4_spmd.clone.sunk | while | flops 68419800 | bytes 2345530 | solution.py:72
  68.6 0.5 select_reduce_fusion.5
  69.1 2.0 collective-permute-start.1
  72.1 2.4 collective-permute-done.2
  74.8 0.5 select_reduce_fusion.5
  76.2 1.9 collective-permute-start.3
  78.4 0.7 collective-permute-done.2
  79.5 0.5 select_reduce_fusion.5
  80.0 2.0 collective-permute-start.1
  83.0 2.4 collective-permute-done.2
  85.8 0.5 select_reduce_fusion.5
  87.1 1.9 collective-permute-start.3
  89.3 0.7 collective-permute-done.2
  90.2 0.5 fusion.29
  90.8 24.9 %while.45 = (s32[]{:T(128)}, bf16[64,256]{1,0:T(8,128)(2,1)S(1)}, f32[64]{0:T(128)S(1)}, f32[64,256]{1,0:T(8,128)S(1)}, f32[2048,256]{1,0:T(8,128)}, /*index=5*/...) while((s32[]{:T(128)}, bf16[64,256]{1,0:T(8,128)(2,1)S(1)}, ...), condition=%wide.region_6.7_spmd.clone, body=%wide.region_5.6_spmd.clone.sunk | while | flops 203980896 | bytes 7744540 | solution.py:104
  90.9 1.9 collective-permute-start.5
  93.0 0.5 fusion.60
  93.9 1.8 fusion.62
  95.7 1.8 collective-permute-done.6
  98.0 0.5 fusion.60
  99.0 3.4 fusion.62
  102.5 1.7 collective-permute-start.4
  104.7 0.5 fusion.60
  105.6 3.4 fusion.62
  109.2 1.7 collective-permute-start.5
  111.2 0.5 fusion.60
  112.2 3.4 fusion.62
  115.8 65.3 %reduce-scatter.2.cloned.1.call-done = f32[256,256]{1,0:T(8,128)} async-done(((f32[2048,256]{1,0:T(8,128)}), f32[256,256]{1,0:T(8,128)}) %reduce-scatter.2.cloned.1.call-update) | async-done | bytes 262160 | tf_op jit(solution)/shard_map/reduce_scatter | solution.py:106
  181.1 3.2 convolution_bitcast_fusion
  184.3 1.5 fusion.24
  185.8 138.1 %all-reduce.3.cloned.1.call-done = (f32[512,1024]{0,1:T(8,128)}, f32[1024,256]{1,0:T(8,128)}) async-done(((f32[512,1024]{0,1:T(8,128)}, f32[1024,256]{1,0:T(8,128)}), (f32[512,1024]{0,1:T(8,128)}, f32[1024,256]{1,0:T(8,128)})) %all-reduce.3.cloned.1.call-update) | async-done | bytes 3145744 | tf_op jit(solution)/shard_map/psum | solution.py:114
  323.9 3.1 broadcast_multiply_fusion
  327.1 3.0 copy.10
  330.1 1.1 broadcast_multiply_fusion.1
  331.1 0.6 copy.61
  (166 shorter events, 10.0 us)
Async XLA Ops:
  7.2 1.2 copy-start
  7.2 2.6 copy-start.9
  7.2 173.9 %reduce-scatter.2.cloned.1.call-start = ((), (), s32[]{:S(2)}) async-start(), calls=%async_computation.1 | async-start | bytes 2359296 | tf_op jit(solution)/shard_map/reduce_scatter | solution.py:106
  8.4 51.4 %copy-start.1 = (bf16[64,256]{1,0:T(8,128)(2,1)}, bf16[64,256]{1,0:T(8,128)(2,1)S(1)}, u32[]{:S(2)}) copy-start(bf16[64,256]{1,0:T(8,128)(2,1)S(1)} %copy.60) | copy-start | bytes 98308
  9.8 1.0 copy-start.4
  10.8 9.5 %collective-permute-start.7 = (bf16[256,256]{1,0:T(8,128)(2,1)S(1)}, bf16[256,256]{1,0:T(8,128)(2,1)S(1)}, u32[]{:S(2)}, u32[]{:S(2)}) collective-permute-start(bf16[256,256]{1,0:T(8,128)(2,1)S(1)} %convolution_convert_fusion), channel_id=1, source_target_pairs={{0,4},{4,8},{8,12},{12,16},{16,20},{20,24},{24,28},{28,0},{1,5},{5... | collective-permute-start | bytes 393224 | tf_op jit(solution)/shard_map/ppermute | solution.py:36
  20.3 7.7 %collective-permute-start.8 = (bf16[256,256]{1,0:T(8,128)(2,1)S(1)}, bf16[256,256]{1,0:T(8,128)(2,1)S(1)}, u32[]{:S(2)}, u32[]{:S(2)}) collective-permute-start(bf16[256,256]{1,0:T(8,128)(2,1)S(1)} %collective-permute-done.7), channel_id=1, source_target_pairs={{0,4},{4,8},{8,12},{12,16},{16,20},{20,24},{24,28},{28,0},{1,5},{5... | collective-permute-start | bytes 393224 | tf_op jit(solution)/shard_map/ppermute | solution.py:36
  28.0 7.7 %collective-permute-start.9 = (bf16[256,256]{1,0:T(8,128)(2,1)S(1)}, bf16[256,256]{1,0:T(8,128)(2,1)S(1)}, u32[]{:S(2)}, u32[]{:S(2)}) collective-permute-start(bf16[256,256]{1,0:T(8,128)(2,1)S(1)} %collective-permute-done.8), channel_id=1, source_target_pairs={{0,4},{4,8},{8,12},{12,16},{16,20},{20,24},{24,28},{28,0},{1,5},{5... | collective-permute-start | bytes 393224 | tf_op jit(solution)/shard_map/ppermute | solution.py:36
  35.6 7.7 %collective-permute-start.10 = (bf16[256,256]{1,0:T(8,128)(2,1)S(1)}, bf16[256,256]{1,0:T(8,128)(2,1)S(1)}, u32[]{:S(2)}, u32[]{:S(2)}) collective-permute-start(bf16[256,256]{1,0:T(8,128)(2,1)S(1)} %collective-permute-done.9), channel_id=1, source_target_pairs={{0,4},{4,8},{8,12},{12,16},{16,20},{20,24},{24,28},{28,0},{1,5},{5... | collective-permute-start | bytes 393224 | tf_op jit(solution)/shard_map/ppermute | solution.py:36
  43.3 7.7 %collective-permute-start.11 = (bf16[256,256]{1,0:T(8,128)(2,1)S(1)}, bf16[256,256]{1,0:T(8,128)(2,1)S(1)}, u32[]{:S(2)}, u32[]{:S(2)}) collective-permute-start(bf16[256,256]{1,0:T(8,128)(2,1)S(1)} %collective-permute-done.10), channel_id=1, source_target_pairs={{0,4},{4,8},{8,12},{12,16},{16,20},{20,24},{24,28},{28,0},{1,5},{5... | collective-permute-start | bytes 393224 | tf_op jit(solution)/shard_map/ppermute | solution.py:36
  51.0 8.8 %collective-permute-start.12 = (bf16[256,256]{1,0:T(8,128)(2,1)S(1)}, bf16[256,256]{1,0:T(8,128)(2,1)S(1)}, u32[]{:S(2)}, u32[]{:S(2)}) collective-permute-start(bf16[256,256]{1,0:T(8,128)(2,1)S(1)} %collective-permute-done.11), channel_id=1, source_target_pairs={{0,4},{4,8},{8,12},{12,16},{16,20},{20,24},{24,28},{28,0},{1,5},{5... | collective-permute-start | bytes 393224 | tf_op jit(solution)/shard_map/ppermute | solution.py:36
  59.8 7.7 %collective-permute-start.13 = (bf16[256,256]{1,0:T(8,128)(2,1)S(1)}, bf16[256,256]{1,0:T(8,128)(2,1)S(1)}, u32[]{:S(2)}, u32[]{:S(2)}) collective-permute-start(bf16[256,256]{1,0:T(8,128)(2,1)S(1)} %collective-permute-done.12), channel_id=1, source_target_pairs={{0,4},{4,8},{8,12},{12,16},{16,20},{20,24},{24,28},{28,0},{1,5},{5... | collective-permute-start | bytes 393224 | tf_op jit(solution)/shard_map/ppermute | solution.py:36
  67.6 0.8 copy-start.3
  67.6 0.8 copy-start.8
  68.4 22.4 %copy-start.2 = (bf16[64,256]{1,0:T(8,128)(2,1)S(1)}, bf16[64,256]{1,0:T(8,128)(2,1)}, u32[]{:S(2)}) copy-start(bf16[64,256]{1,0:T(8,128)(2,1)} %copy-done.1) | copy-start | bytes 98308
  68.4 6.3 %collective-permute-start = (bf16[64,256]{1,0:T(8,128)(2,1)S(1)}, bf16[64,256]{1,0:T(8,128)(2,1)S(1)}, u32[]{:S(2)}, u32[]{:S(2)}) collective-permute-start(bf16[64,256]{1,0:T(8,128)(2,1)S(1)} %copy.32), channel_id=1, source_target_pairs={{0,1},{1,2},{2,3},{3,0},{4,5},{5,6},{6,7},{7,4},{8,9},{9,10},{10,1... | collective-permute-start | bytes 98312 | tf_op jit(solution)/shard_map/while/body/eval_jaxpr/ppermute | solution.py:10
  69.1 3.0 collective-permute-start.1
  71.5 3.0 collective-permute-start.2
  71.6 3.1 collective-permute-start.3
  74.7 4.6 %collective-permute-start = (bf16[64,256]{1,0:T(8,128)(2,1)S(1)}, bf16[64,256]{1,0:T(8,128)(2,1)S(1)}, u32[]{:S(2)}, u32[]{:S(2)}) collective-permute-start(bf16[64,256]{1,0:T(8,128)(2,1)S(1)} %copy.32), channel_id=1, source_target_pairs={{0,1},{1,2},{2,3},{3,0},{4,5},{5,6},{6,7},{7,4},{8,9},{9,10},{10,1... | collective-permute-start | bytes 98312 | tf_op jit(solution)/shard_map/while/body/eval_jaxpr/ppermute | solution.py:10
  75.4 3.0 collective-permute-start.1
  76.1 3.0 collective-permute-start.2
  76.2 3.1 collective-permute-start.3
  79.3 6.3 %collective-permute-start = (bf16[64,256]{1,0:T(8,128)(2,1)S(1)}, bf16[64,256]{1,0:T(8,128)(2,1)S(1)}, u32[]{:S(2)}, u32[]{:S(2)}) collective-permute-start(bf16[64,256]{1,0:T(8,128)(2,1)S(1)} %copy.32), channel_id=1, source_target_pairs={{0,1},{1,2},{2,3},{3,0},{4,5},{5,6},{6,7},{7,4},{8,9},{9,10},{10,1... | collective-permute-start | bytes 98312 | tf_op jit(solution)/shard_map/while/body/eval_jaxpr/ppermute | solution.py:10
  80.0 3.0 collective-permute-start.1
  82.4 3.0 collective-permute-start.2
  82.5 3.1 collective-permute-start.3
  85.6 4.6 %collective-permute-start = (bf16[64,256]{1,0:T(8,128)(2,1)S(1)}, bf16[64,256]{1,0:T(8,128)(2,1)S(1)}, u32[]{:S(2)}, u32[]{:S(2)}) collective-permute-start(bf16[64,256]{1,0:T(8,128)(2,1)S(1)} %copy.32), channel_id=1, source_target_pairs={{0,1},{1,2},{2,3},{3,0},{4,5},{5,6},{6,7},{7,4},{8,9},{9,10},{10,1... | collective-permute-start | bytes 98312 | tf_op jit(solution)/shard_map/while/body/eval_jaxpr/ppermute | solution.py:10
  86.3 3.0 collective-permute-start.1
  87.0 3.0 collective-permute-start.2
  87.1 3.1 collective-permute-start.3
  90.8 4.9 %collective-permute-start.4 = (bf16[64,256]{1,0:T(8,128)(2,1)S(1)}, bf16[64,256]{1,0:T(8,128)(2,1)S(1)}, u32[]{:S(2)}, u32[]{:S(2)}) collective-permute-start(bf16[64,256]{1,0:T(8,128)(2,1)S(1)} %copy.47), channel_id=1, source_target_pairs={{0,1},{1,2},{2,3},{3,0},{4,5},{5,6},{6,7},{7,4},{8,9},{9,10},{10,1... | collective-permute-start | bytes 98312 | tf_op jit(solution)/shard_map/while/body/eval_jaxpr/ppermute | solution.py:10
  90.9 4.8 %collective-permute-start.5 = (f32[64]{0:T(128)S(1)}, f32[64]{0:T(128)S(1)}, u32[]{:S(2)}, u32[]{:S(2)}) collective-permute-start(f32[64]{0:T(128)S(1)} %copy.48), channel_id=1, source_target_pairs={{0,1},{1,2},{2,3},{3,0},{4,5},{5,6},{6,7},{7,4},{8,9},{9,10},{10,1... | collective-permute-start | bytes 776 | tf_op jit(solution)/shard_map/while/body/eval_jaxpr/ppermute | solution.py:10
  93.8 3.7 %collective-permute-start.6 = (f32[64,256]{1,0:T(8,128)S(1)}, f32[64,256]{1,0:T(8,128)S(1)}, u32[]{:S(2)}, u32[]{:S(2)}) collective-permute-start(f32[64,256]{1,0:T(8,128)S(1)} %fusion.61), channel_id=1, source_target_pairs={{0,1},{1,2},{2,3},{3,0},{4,5},{5,6},{6,7},{7,4},{8,9},{9,10},{10,1... | collective-permute-start | bytes 196616 | tf_op jit(solution)/shard_map/while/body/eval_jaxpr/ppermute | solution.py:10
  97.5 4.8 %collective-permute-start.4 = (bf16[64,256]{1,0:T(8,128)(2,1)S(1)}, bf16[64,256]{1,0:T(8,128)(2,1)S(1)}, u32[]{:S(2)}, u32[]{:S(2)}) collective-permute-start(bf16[64,256]{1,0:T(8,128)(2,1)S(1)} %copy.47), channel_id=1, source_target_pairs={{0,1},{1,2},{2,3},{3,0},{4,5},{5,6},{6,7},{7,4},{8,9},{9,10},{10,1... | collective-permute-start | bytes 98312 | tf_op jit(solution)/shard_map/while/body/eval_jaxpr/ppermute | solution.py:10
  97.5 4.8 %collective-permute-start.5 = (f32[64]{0:T(128)S(1)}, f32[64]{0:T(128)S(1)}, u32[]{:S(2)}, u32[]{:S(2)}) collective-permute-start(f32[64]{0:T(128)S(1)} %copy.48), channel_id=1, source_target_pairs={{0,1},{1,2},{2,3},{3,0},{4,5},{5,6},{6,7},{7,4},{8,9},{9,10},{10,1... | collective-permute-start | bytes 776 | tf_op jit(solution)/shard_map/while/body/eval_jaxpr/ppermute | solution.py:10
  98.8 3.7 %collective-permute-start.6 = (f32[64,256]{1,0:T(8,128)S(1)}, f32[64,256]{1,0:T(8,128)S(1)}, u32[]{:S(2)}, u32[]{:S(2)}) collective-permute-start(f32[64,256]{1,0:T(8,128)S(1)} %fusion.61), channel_id=1, source_target_pairs={{0,1},{1,2},{2,3},{3,0},{4,5},{5,6},{6,7},{7,4},{8,9},{9,10},{10,1... | collective-permute-start | bytes 196616 | tf_op jit(solution)/shard_map/while/body/eval_jaxpr/ppermute | solution.py:10
  102.5 6.4 %collective-permute-start.4 = (bf16[64,256]{1,0:T(8,128)(2,1)S(1)}, bf16[64,256]{1,0:T(8,128)(2,1)S(1)}, u32[]{:S(2)}, u32[]{:S(2)}) collective-permute-start(bf16[64,256]{1,0:T(8,128)(2,1)S(1)} %copy.47), channel_id=1, source_target_pairs={{0,1},{1,2},{2,3},{3,0},{4,5},{5,6},{6,7},{7,4},{8,9},{9,10},{10,1... | collective-permute-start | bytes 98312 | tf_op jit(solution)/shard_map/while/body/eval_jaxpr/ppermute | solution.py:10
  104.2 4.7 %collective-permute-start.5 = (f32[64]{0:T(128)S(1)}, f32[64]{0:T(128)S(1)}, u32[]{:S(2)}, u32[]{:S(2)}) collective-permute-start(f32[64]{0:T(128)S(1)} %copy.48), channel_id=1, source_target_pairs={{0,1},{1,2},{2,3},{3,0},{4,5},{5,6},{6,7},{7,4},{8,9},{9,10},{10,1... | collective-permute-start | bytes 776 | tf_op jit(solution)/shard_map/while/body/eval_jaxpr/ppermute | solution.py:10
  105.4 3.7 %collective-permute-start.6 = (f32[64,256]{1,0:T(8,128)S(1)}, f32[64,256]{1,0:T(8,128)S(1)}, u32[]{:S(2)}, u32[]{:S(2)}) collective-permute-start(f32[64,256]{1,0:T(8,128)S(1)} %fusion.61), channel_id=1, source_target_pairs={{0,1},{1,2},{2,3},{3,0},{4,5},{5,6},{6,7},{7,4},{8,9},{9,10},{10,1... | collective-permute-start | bytes 196616 | tf_op jit(solution)/shard_map/while/body/eval_jaxpr/ppermute | solution.py:10
  109.2 6.4 %collective-permute-start.4 = (bf16[64,256]{1,0:T(8,128)(2,1)S(1)}, bf16[64,256]{1,0:T(8,128)(2,1)S(1)}, u32[]{:S(2)}, u32[]{:S(2)}) collective-permute-start(bf16[64,256]{1,0:T(8,128)(2,1)S(1)} %copy.47), channel_id=1, source_target_pairs={{0,1},{1,2},{2,3},{3,0},{4,5},{5,6},{6,7},{7,4},{8,9},{9,10},{10,1... | collective-permute-start | bytes 98312 | tf_op jit(solution)/shard_map/while/body/eval_jaxpr/ppermute | solution.py:10
  109.2 6.4 %collective-permute-start.5 = (f32[64]{0:T(128)S(1)}, f32[64]{0:T(128)S(1)}, u32[]{:S(2)}, u32[]{:S(2)}) collective-permute-start(f32[64]{0:T(128)S(1)} %copy.48), channel_id=1, source_target_pairs={{0,1},{1,2},{2,3},{3,0},{4,5},{5,6},{6,7},{7,4},{8,9},{9,10},{10,1... | collective-permute-start | bytes 776 | tf_op jit(solution)/shard_map/while/body/eval_jaxpr/ppermute | solution.py:10
  111.9 3.7 %collective-permute-start.6 = (f32[64,256]{1,0:T(8,128)S(1)}, f32[64,256]{1,0:T(8,128)S(1)}, u32[]{:S(2)}, u32[]{:S(2)}) collective-permute-start(f32[64,256]{1,0:T(8,128)S(1)} %fusion.61), channel_id=1, source_target_pairs={{0,1},{1,2},{2,3},{3,0},{4,5},{5,6},{6,7},{7,4},{8,9},{9,10},{10,1... | collective-permute-start | bytes 196616 | tf_op jit(solution)/shard_map/while/body/eval_jaxpr/ppermute | solution.py:10
  115.7 65.4 %copy-start.5 = (f32[256,1024]{1,0:T(8,128)S(1)}, f32[256,1024]{1,0:T(8,128)}, u32[]{:S(2)}) copy-start(f32[256,1024]{1,0:T(8,128)} %copy-done.4) | copy-start | bytes 3145732
  115.7 65.4 %copy-start.7 = (bf16[1,256,512]{2,1,0:T(8,128)(2,1)S(1)}, bf16[1,256,512]{2,1,0:T(8,128)(2,1)}, u32[]{:S(2)}) copy-start(bf16[1,256,512]{2,1,0:T(8,128)(2,1)} %param.13) | copy-start | bytes 786436
  115.7 208.2 %all-reduce.3.cloned.1.call-start = ((), (), s32[]{:S(2)}) async-start(), calls=%async_computation.2 | async-start | bytes 6291456 | tf_op jit(solution)/shard_map/psum | solution.py:114
  181.1 3.2 copy-start.10
  327.1 3.0 copy-start.6
  (1 other events, 0.7 us)
Sparse Core Ops, SparseCore 0:
  115.8 65.2 reduce-scatter.1
  187.2 136.6 all-reduce.2
